TPU v7x, 32 devices: a whole 2x2x4 slice. The times are simulated.
32 devices in a mesh: rows: 8 (over y, x, core), sub: 4 (over z).
Axes of the slice: x: 2, y: 2, z: 4, core: 2. Of those that a mesh axis runs over, the one named last changes fastest.
Arguments:
- old_basis: bfloat16 [32, 524288], P(None, ('rows', 'sub')), may hold values from -1 to 1
- snapshots: bfloat16 [512, 524288], P(None, ('rows', 'sub')), may hold values from -16 to 16
- gap_flags: int32 [512, 4096], P(None, ('rows', 'sub')), may hold values from 0 to 1, as said below
- sketch_seed: int32 [512, 64], replicated, may hold values from -1 to 1
Outputs:
- new_basis: float32 [32, 524288], P(None, ('rows', 'sub'))
- coefficients: float32 [32, 512], replicated
Inputs may be any that keep to these rules, and one draw needn't show every extreme that they name: `gap_flags`: 1 marks a block of 128 velocity rows measured in that snapshot, 0 a gap; every snapshot has measured blocks and gaps.
All inputs are finite; a program needn't handle non-finite values.
Results may differ from a plain program's by a relative error of at most 0.00135.
The roundings to bfloat16 on the way count: a program that leaves them out, or rounds other values in their place, can miss the bound.
Values may be sent and summed in bfloat16 or wider, within the bound.
No kernel may reach another device: no remote copies, remote signals or barrier semaphores. Data moves between devices by JAX's collectives and lax.ppermute only.
A program may use at most 192 MiB of HBM per device.

v0:
```python
import math
import jax
import jax.numpy as jnp
from jax import lax
from jax.sharding import PartitionSpec as P

POWER = 2
damping = 0.005
highest = lax.Precision.HIGHEST


def cholesky_last(system):
    extent = system.shape[0]
    factor = jnp.zeros_like(system)
    for column in range(extent):
        partial_sum = jnp.sum(factor * factor[column : column + 1], axis=1)
        remain = system[:, column] - partial_sum
        diagonal_root = jnp.sqrt(remain[column])
        lower_part = (jnp.arange(extent) >= column).reshape((extent,) + (1,) * (system.ndim - 2))
        factor = factor.at[:, column].set(jnp.where(lower_part, remain / diagonal_root, 0.0))
    return factor


def lower_solve(factor, target):
    extent = factor.shape[0]
    result = jnp.zeros_like(target)
    for column in range(extent):
        current = (target[column] - jnp.sum(factor[column] * result, axis=0)) / factor[
            column, column
        ]
        result = result.at[column].set(current)
    return result


def upper_solve(factor, target):
    extent = factor.shape[0]
    result = jnp.zeros_like(target)
    for column in reversed(range(extent)):
        current = (target[column] - jnp.sum(factor[:, column] * result, axis=0)) / factor[
            column, column
        ]
        result = result.at[column].set(current)
    return result


def solve_normal(grams, right, modes, rows_all):
    snapshot_count = grams.shape[0]
    identity = jnp.eye(modes, dtype=jnp.float32)[:, :, None]
    system = grams.T.reshape(modes, modes, snapshot_count) + damping * rows_all * identity
    factor = cholesky_last(system)
    return upper_solve(factor, lower_solve(factor, right.T))


def inverse_factor(products):
    extent = products.shape[0]
    factor = cholesky_last(products[:, :, None])
    return lower_solve(factor, jnp.eye(extent, dtype=jnp.float32))


def mask_blocks(samples, flag_blocks):
    snapshot_count, blocks_dev = flag_blocks.shape
    weights = flag_blocks.astype(samples.dtype)[:, :, None]
    return (samples.reshape(snapshot_count, blocks_dev, -1) * weights).reshape(snapshot_count, -1)


def refill(samples, flag_blocks, recon_low):
    snapshot_count, blocks_dev = flag_blocks.shape
    observed = (flag_blocks > 0)[:, :, None]
    combined = jnp.where(
        observed,
        samples.reshape(snapshot_count, blocks_dev, -1),
        recon_low.reshape(snapshot_count, blocks_dev, -1),
    )
    return combined.reshape(snapshot_count, -1)


def contract_rows(former, latter):
    return lax.dot_general(
        former, latter, (((1,), (1,)), ((), ())), preferred_element_type=jnp.float32
    )


def contract_first(former, latter):
    return lax.dot_general(
        former, latter, (((0,), (0,)), ((), ())), preferred_element_type=jnp.float32
    )


def per_device(old_basis, snapshots, gap_flags, sketch_seed):
    modes = old_basis.shape[0]
    rows_all = old_basis.shape[1] * lax.axis_size(("rows", "sub"))
    blocks_dev = gap_flags.shape[1]
    masked = mask_blocks(snapshots, gap_flags)
    right = contract_rows(masked, old_basis)
    pieces = old_basis.reshape(modes, blocks_dev, -1)
    block_grams = jnp.einsum("kbi,lbi->bkl", pieces, pieces, preferred_element_type=jnp.float32)
    block_rows = block_grams.reshape(blocks_dev, modes * modes)
    grams = jnp.dot(gap_flags.astype(jnp.float32), block_rows, precision=highest)
    mixer = sketch_seed.astype(jnp.bfloat16)
    gram_total, right_total = lax.psum((grams, right), ("rows", "sub"))
    coefficients = solve_normal(gram_total, right_total, modes, rows_all)
    recon_low = contract_first(coefficients.astype(jnp.bfloat16), old_basis).astype(jnp.bfloat16)
    filled = refill(snapshots, gap_flags, recon_low)
    sketch = contract_first(mixer, filled)
    inverse = None
    for sweep_index in range(POWER + 1):
        if sweep_index > 0:
            sketch = contract_first(mixer, filled)
        local_gram = lax.dot_general(
            sketch,
            sketch,
            (((1,), (1,)), ((), ())),
            precision=highest,
            preferred_element_type=jnp.float32,
        )
        products = lax.psum(local_gram, ("rows", "sub"))
        inverse = inverse_factor(products)
        if sweep_index < POWER:
            ortho_rows = jnp.dot(inverse, sketch, precision=highest).astype(jnp.bfloat16)
            mixer_share = lax.psum_scatter(
                contract_rows(filled, ortho_rows), ("rows", "sub"), scatter_dimension=0, tiled=True
            ).astype(jnp.bfloat16)
            mixer = lax.all_gather(mixer_share, ("rows", "sub"), axis=0, tiled=True)
    root_rows = math.sqrt(rows_all)
    new_basis = jnp.dot(inverse[:modes], sketch, precision=highest) * root_rows
    return (new_basis, coefficients)


def solution(mesh):
    in_specs = (P(None, ("rows", "sub")), P(None, ("rows", "sub")), P(None, ("rows", "sub")), P())
    out_specs = (P(None, ("rows", "sub")), P())
    return jax.shard_map(
        per_device, mesh=mesh, in_specs=in_specs, out_specs=out_specs, check_vma=False
    )
```

profile of v0, /device:TPU:0, one launch (start us, length us, event | category | flops | bytes accessed | tf_op | source)
XLA Modules:
  0.0 1549.7 jit_solution(17264317991794373059)
XLA Ops:
  9.1 2.1 copy.518
  11.2 2.8 fusion.6
  14.1 2.5 copy.519
  16.6 13.0 mul.4308
  29.6 24.4 %fusion.2 = f32[32,512]{1,0:T(8,128)} fusion(bf16[32,16384]{1,0:T(8,128)(2,1)S(1)} %copy-done, bf16[512,16384]{1,0:T(8,128)(2,1)} %param.965, bf16[64,8,128,128]{3,2,1,0:T(8,128)(2,1)} %bitcast.3922), kind=kOutput, calls=%fused_computation.40 | convolution fusion | flops 545259520 | bytes 34668544 | tf_op jit(solution)/shard_map/dot_general | solution.py:78
  54.7 137.0 %all-reduce.12.cloned.1.call-done = (f32[32,32,512]{2,0,1:T(8,128)}, f32[32,512]{1,0:T(8,128)}) async-done(((f32[32,32,512]{2,0,1:T(8,128)}, f32[32,512]{1,0:T(8,128)}), (f32[32,32,512]{2,0,1:T(8,128)}, f32[32,512]{1,0:T(8,128)})) %all-reduce.12.cloned.1.call-update) | async-done | bytes 2162704 | tf_op jit(solution)/shard_map/psum | solution.py:100
  191.7 1.8 broadcast_add_fusion
  291.6 12.0 broadcast_in_dim.635
  303.5 15.2 bitcast_select_fusion
  318.8 8.8 fusion.224
  327.6 1.9 copy-done.5
  329.5 3.4 convolution_bitcast_fusion.2
  332.9 39.6 %psum.37 = f32[64,64,1]{1,0,2:T(8,128)S(1)} all-reduce(f32[64,64,1]{1,0,2:T(8,128)S(1)} %convolution_bitcast_fusion.2), channel_id=1, replica_groups=mesh['rows'=8,'sub'=4] {'rows','sub'}, use_global_device_ids=true, to_apply=%region_97.98 | all-reduce | flops 4096 | bytes 32768 | tf_op jit(solution)/shard_map/psum | solution.py:116
  581.6 6.0 convolution_convert_fusion.2
  587.6 8.8 fusion.526
  596.5 133.4 %reduce-scatter.3.cloned.1.call-done = f32[16,64]{1,0:T(8,128)} async-done(((f32[512,64]{1,0:T(8,128)}), f32[16,64]{1,0:T(8,128)}) %reduce-scatter.3.cloned.1.call-update) | async-done | bytes 4112 | tf_op jit(solution)/shard_map/reduce_scatter | solution.py:120
  730.6 64.8 %all_gather.6 = bf16[512,64]{1,0:T(8,128)(2,1)S(1)} all-gather(bf16[16,64]{1,0:T(8,128)(2,1)S(1)} %convert_element_type.415), channel_id=1, replica_groups=mesh['rows'=8,'sub'=4] {'rows','sub'}, dimensions={0}, use_global_device_ids=true | all-gather | bytes 67584 | tf_op jit(solution)/shard_map/all_gather | solution.py:123
  795.3 8.9 fusion.527
  804.2 1.9 copy-done.4
  806.2 3.4 convolution_bitcast_fusion.1
  809.6 39.9 %psum.38 = f32[64,64,1]{1,0,2:T(8,128)S(1)} all-reduce(f32[64,64,1]{1,0,2:T(8,128)S(1)} %convolution_bitcast_fusion.1), channel_id=1, replica_groups=mesh['rows'=8,'sub'=4] {'rows','sub'}, use_global_device_ids=true, to_apply=%region_226.227 | all-reduce | flops 4096 | bytes 32768 | tf_op jit(solution)/shard_map/psum | solution.py:116
  970.7 1.9 subtract_divide_fusion.3
  1062.7 6.0 convolution_convert_fusion.1
  1068.7 8.8 fusion.528
  1077.5 133.0 %reduce-scatter.5.cloned.1.call-done = f32[16,64]{1,0:T(8,128)} async-done(((f32[512,64]{1,0:T(8,128)}), f32[16,64]{1,0:T(8,128)}) %reduce-scatter.5.cloned.1.call-update) | async-done | bytes 4112 | tf_op jit(solution)/shard_map/reduce_scatter | solution.py:120
  1211.2 64.8 %all_gather.7 = bf16[512,64]{1,0:T(8,128)(2,1)S(1)} all-gather(bf16[16,64]{1,0:T(8,128)(2,1)S(1)} %convert_element_type.417), channel_id=1, replica_groups=mesh['rows'=8,'sub'=4] {'rows','sub'}, dimensions={0}, use_global_device_ids=true | all-gather | bytes 67584 | tf_op jit(solution)/shard_map/all_gather | solution.py:123
  1276.0 8.9 fusion.529
  1284.9 1.9 copy-done.3
  1286.8 3.4 convolution_bitcast_fusion
  1290.2 39.9 %psum.39 = f32[64,64,1]{1,0,2:T(8,128)S(1)} all-reduce(f32[64,64,1]{1,0,2:T(8,128)S(1)} %convolution_bitcast_fusion), channel_id=1, replica_groups=mesh['rows'=8,'sub'=4] {'rows','sub'}, use_global_device_ids=true, to_apply=%region_355.356 | all-reduce | flops 4096 | bytes 32768 | tf_op jit(solution)/shard_map/psum | solution.py:116
  1450.6 1.9 subtract_divide_fusion.2
  1537.1 5.7 convolution_multiply_fusion
  (2334 shorter events, 587.0 us)
Async XLA Ops:
  7.2 1.3 copy-start
  7.2 184.5 %all-reduce.12.cloned.1.call-start = ((), (), s32[]{:S(2)}) async-start(), calls=%async_computation.4 | async-start | bytes 4325376 | tf_op jit(solution)/shard_map/psum | solution.py:100
  9.1 2.1 copy-start.8
  54.0 675.8 %reduce-scatter.3.cloned.1.call-start = ((), (), s32[]{:S(2)}) async-start(), calls=%async_computation.2 | async-start | bytes 270336 | tf_op jit(solution)/shard_map/reduce_scatter | solution.py:120
  54.7 443.3 %copy-start.9 = (f32[64,64]{1,0:T(8,128)}, f32[64,64]{1,0:T(8,128)S(1)}, u32[]{:S(2)}) copy-start(f32[64,64]{1,0:T(8,128)S(1)} %fusion.228) | copy-start | bytes 49156
  210.1 2.8 copy-start.2
  238.2 3.3 copy-start.6
  291.5 12.0 copy-start.7
  303.5 15.2 copy-start.10
  327.5 1.9 copy-start.5
  596.4 614.1 %reduce-scatter.5.cloned.1.call-start = ((), (), s32[]{:S(2)}) async-start(), calls=%async_computation.3 | async-start | bytes 270336 | tf_op jit(solution)/shard_map/reduce_scatter | solution.py:120
  804.2 1.9 copy-start.4
  1284.9 1.9 copy-start.3
  1537.0 5.7 copy-start.1
Sparse Core Ops, SparseCore 0:
  54.2 137.4 all-reduce.11
  596.5 133.2 reduce-scatter.2
  1077.6 132.8 reduce-scatter.4
where the time goes:
time: 1580 us; the launch traced here: 1550 us
  waiting for transfers between devices  403 us (26%)
  other arithmetic  392 us (25%)
  blocking collectives  249 us (16%)
  local copies, waits for them, and re-layouts  234 us (15%)
  between operations  155 us (10%)
  matrix products  115 us (7%)
    div x219, other arithmetic, lower_solve(): (target[column] - jnp.sum(factor[column] * result, axis=0)) / factor[colu...  267 us
    reduce_scatter x2, waiting for transfers between devices, per_device(): lax.psum_scatter(contract_rows(filled, ortho_rows), ('rows', 'sub'), scat...  266 us
    psum x1, waiting for transfers between devices, per_device(): gram_total, right_total = lax.psum((grams, right), ('rows', 'sub'))  137 us
    all_gather x2, blocking collectives, per_device(): mixer = lax.all_gather(mixer_share, ('rows', 'sub'), axis=0, tiled=True)  130 us
    psum x3, blocking collectives, per_device(): products = lax.psum(local_gram, ('rows', 'sub'))  119 us
    slice x192, local copies, waits for them, and re-layouts, cholesky_last(): diagonal_root = jnp.sqrt(remain[column])  113 us
    dot_general x3, matrix products, contract_rows(): lax.dot_general(former, latter, (((1,), (1,)), ((), ())), preferred_eleme...  42 us
    dot_general x4, matrix products, contract_first(): lax.dot_general(former, latter, (((0,), (0,)), ((), ())), preferred_eleme...  41.8 us
  transfers between devices with their start and end apart: 3, of which 3 were waited for; matrix products, arithmetic and copies ran while one was open for 0% of the time, Pallas kernels for 0%

commit v1 on v0

--- a/solution.py
+++ b/solution.py
@@ -7,6 +7,27 @@
 POWER = 2
 damping = 0.005
 highest = lax.Precision.HIGHEST
+
+
+def in_order(parts, dim):
+    parts = jnp.moveaxis(parts, 0, dim)
+    lengths = parts.shape
+    return parts.reshape(*lengths[:dim], lengths[dim] * lengths[dim + 1], *lengths[dim + 2 :])
+
+
+def collected_by_bits(x, axis):
+    size, mine = (lax.axis_size(axis), lax.axis_index(axis))
+    blocks, bit = (x[None], 1)
+    while bit < size:
+        other = lax.ppermute(blocks, axis, [(i, i ^ bit) for i in range(size)])
+        low = mine & bit == 0
+        blocks = jnp.concatenate([jnp.where(low, blocks, other), jnp.where(low, other, blocks)])
+        bit *= 2
+    return blocks
+
+
+def gather_by_bits(value, axis, dim):
+    return in_order(collected_by_bits(value, axis), dim)
 
 
 def cholesky_last(system):
@@ -120,7 +141,7 @@
             mixer_share = lax.psum_scatter(
                 contract_rows(filled, ortho_rows), ("rows", "sub"), scatter_dimension=0, tiled=True
             ).astype(jnp.bfloat16)
-            mixer = lax.all_gather(mixer_share, ("rows", "sub"), axis=0, tiled=True)
+            mixer = gather_by_bits(mixer_share, ("rows", "sub"), 0)
     root_rows = math.sqrt(rows_all)
     new_basis = jnp.dot(inverse[:modes], sketch, precision=highest) * root_rows
     return (new_basis, coefficients)

time: 1580 us -> 1480 us (0.937)
  blocking collectives: 249 us -> 115 us
  waiting for transfers between devices: 403 us -> 438 us
    all_gather x2 -> x0, blocking collectives: 130 us -> none  [per_device(): mixer = lax.all_gather(mixer_share, ('rows', 'sub'), axis=0, tiled=True)]
    ppermute x0 -> x10, waiting for transfers between devices: none -> 33.8 us  [collected_by_bits(): other = lax.ppermute(blocks, axis, [(i, i ^ bit) for i in range(size)])]
  transfers between devices with their start and end apart: 3 -> 13, of which waited for: 3 -> 13; matrix products, arithmetic and copies ran while one was open for 0% -> 0% of each run, Pallas kernels for 0% -> 0%
where the time goes in v1:
time: 1480 us; the launch traced here: 1450 us
  waiting for transfers between devices  438 us (30%)
  other arithmetic  394 us (27%)
  local copies, waits for them, and re-layouts  234 us (16%)
  between operations  155 us (10%)
  matrix products  116 us (8%)
  blocking collectives  115 us (8%)
    div x219, other arithmetic, lower_solve(): (target[column] - jnp.sum(factor[column] * result, axis=0)) / factor[colu...  267 us
    reduce_scatter x2, waiting for transfers between devices, per_device(): lax.psum_scatter(contract_rows(filled, ortho_rows), ('rows', 'sub'), scat...  267 us
    psum x1, waiting for transfers between devices, per_device(): gram_total, right_total = lax.psum((grams, right), ('rows', 'sub'))  137 us
    psum x3, blocking collectives, per_device(): products = lax.psum(local_gram, ('rows', 'sub'))  115 us
    slice x192, local copies, waits for them, and re-layouts, cholesky_last(): diagonal_root = jnp.sqrt(remain[column])  113 us
    dot_general x3, matrix products, contract_rows(): lax.dot_general(former, latter, (((1,), (1,)), ((), ())), preferred_eleme...  42.4 us
    dot_general x4, matrix products, contract_first(): lax.dot_general(former, latter, (((0,), (0,)), ((), ())), preferred_eleme...  41.8 us
    scatter x192, local copies, waits for them, and re-layouts, cholesky_last(): factor.at[:, column].set(jnp.where(lower_part, remain / diagonal_root, 0.0))  39.3 us
  transfers between devices with their start and end apart: 13, of which 13 were waited for; matrix products, arithmetic and copies ran while one was open for 0% of the time, Pallas kernels for 0%

profile of v1, /device:TPU:0, one launch (start us, length us, event | category | flops | bytes accessed | tf_op | source)
XLA Modules:
  0.0 1453.7 jit_solution(5655872848497916503)
XLA Ops:
  9.1 2.1 copy.518
  11.2 2.8 fusion.6
  14.1 2.5 copy.519
  16.6 12.6 mul.4313
  29.2 24.4 %fusion.2 = f32[32,512]{1,0:T(8,128)} fusion(bf16[32,16384]{1,0:T(8,128)(2,1)S(1)} %copy-done, bf16[512,16384]{1,0:T(8,128)(2,1)} %param.965, bf16[64,8,128,128]{3,2,1,0:T(8,128)(2,1)} %bitcast.3932), kind=kOutput, calls=%fused_computation.40 | convolution fusion | flops 545259520 | bytes 34668544 | tf_op jit(solution)/shard_map/dot_general | solution.py:99
  54.4 137.0 %all-reduce.12.cloned.1.call-done = (f32[32,32,512]{2,0,1:T(8,128)}, f32[32,512]{1,0:T(8,128)}) async-done(((f32[32,32,512]{2,0,1:T(8,128)}, f32[32,512]{1,0:T(8,128)}), (f32[32,32,512]{2,0,1:T(8,128)}, f32[32,512]{1,0:T(8,128)})) %all-reduce.12.cloned.1.call-update) | async-done | bytes 2162704 | tf_op jit(solution)/shard_map/psum | solution.py:121
  291.3 12.0 broadcast_in_dim.641
  303.2 15.2 %bitcast_select_fusion = bf16[512,16384]{1,0:T(8,128)(2,1)} fusion(bf16[512,16384]{1,0:T(8,128)(2,1)} %param.965, pred[64,8,128,128]{3,2,1,0:T(32,128)(4,1)} %bitcast.3933, bf16[32,16384]{1,0:T(8,128)(2,1)S(1)} %copy-done, f32[32,512]{1,0:T(8,128)S(1)} %scatter.1740), kind=kOutput, calls=%fused_computation | convolution fusion | flops 553664512 | bytes 43057152 | tf_op jit(solution)/shard_map/dot_general | solution.py:105
  318.4 8.8 fusion.224
  329.1 3.4 convolution_bitcast_fusion.2
  332.5 39.5 %psum.37 = f32[64,64,1]{1,0,2:T(8,128)S(1)} all-reduce(f32[64,64,1]{1,0,2:T(8,128)S(1)} %convolution_bitcast_fusion.2), channel_id=1, replica_groups=mesh['rows'=8,'sub'=4] {'rows','sub'}, use_global_device_ids=true, to_apply=%region_97.98 | all-reduce | flops 4096 | bytes 32768 | tf_op jit(solution)/shard_map/psum | solution.py:137
  581.3 6.0 convolution_convert_fusion.2
  587.2 8.8 fusion.526
  596.5 133.1 %reduce-scatter.3.cloned.1.call-done = f32[16,64]{1,0:T(8,128)} async-done(((f32[512,64]{1,0:T(8,128)}), f32[16,64]{1,0:T(8,128)}) %reduce-scatter.3.cloned.1.call-update) | async-done | bytes 4112 | tf_op jit(solution)/shard_map/reduce_scatter | solution.py:141
  730.3 3.6 collective-permute-done
  734.7 4.5 collective-permute-done.1
  740.6 3.9 collective-permute-done.3
  745.1 3.7 collective-permute-done.4
  748.9 8.9 fusion.527
  759.8 3.4 convolution_bitcast_fusion.1
  763.2 37.9 %psum.38 = f32[64,64,1]{1,0,2:T(8,128)S(1)} all-reduce(f32[64,64,1]{1,0,2:T(8,128)S(1)} %convolution_bitcast_fusion.1), channel_id=1, replica_groups=mesh['rows'=8,'sub'=4] {'rows','sub'}, use_global_device_ids=true, to_apply=%region_226.227 | all-reduce | flops 4096 | bytes 32768 | tf_op jit(solution)/shard_map/psum | solution.py:137
  1014.1 6.0 convolution_convert_fusion.1
  1020.1 9.2 fusion.528
  1029.3 133.6 %reduce-scatter.5.cloned.1.call-done = f32[16,64]{1,0:T(8,128)} async-done(((f32[512,64]{1,0:T(8,128)}), f32[16,64]{1,0:T(8,128)}) %reduce-scatter.5.cloned.1.call-update) | async-done | bytes 4112 | tf_op jit(solution)/shard_map/reduce_scatter | solution.py:141
  1163.6 3.6 collective-permute-done.5
  1167.9 4.5 collective-permute-done.6
  1173.9 3.9 collective-permute-done.8
  1178.4 3.7 collective-permute-done.9
  1182.2 8.9 fusion.529
  1193.1 3.4 convolution_bitcast_fusion
  1196.5 37.9 %psum.39 = f32[64,64,1]{1,0,2:T(8,128)S(1)} all-reduce(f32[64,64,1]{1,0,2:T(8,128)S(1)} %convolution_bitcast_fusion), channel_id=1, replica_groups=mesh['rows'=8,'sub'=4] {'rows','sub'}, use_global_device_ids=true, to_apply=%region_355.356 | all-reduce | flops 4096 | bytes 32768 | tf_op jit(solution)/shard_map/psum | solution.py:137
  1441.2 5.7 convolution_multiply_fusion
  (2372 shorter events, 604.2 us)
Async XLA Ops:
  7.2 1.3 copy-start
  7.2 184.2 %all-reduce.12.cloned.1.call-start = ((), (), s32[]{:S(2)}) async-start(), calls=%async_computation.4 | async-start | bytes 4325376 | tf_op jit(solution)/shard_map/psum | solution.py:121
  9.1 2.1 copy-start.8
  53.7 675.9 %reduce-scatter.3.cloned.1.call-start = ((), (), s32[]{:S(2)}) async-start(), calls=%async_computation.2 | async-start | bytes 270336 | tf_op jit(solution)/shard_map/reduce_scatter | solution.py:141
  54.4 443.3 %copy-start.9 = (f32[64,64]{1,0:T(8,128)}, f32[64,64]{1,0:T(8,128)S(1)}, u32[]{:S(2)}) copy-start(f32[64,64]{1,0:T(8,128)S(1)} %fusion.228) | copy-start | bytes 49156
  210.1 2.8 copy-start.2
  238.2 3.3 copy-start.6
  291.2 12.0 copy-start.7
  303.2 15.2 %copy-start.10 = (s32[512,64]{0,1:T(8,128)S(1)}, s32[512,64]{0,1:T(8,128)}, u32[]{:S(2)}) copy-start(s32[512,64]{0,1:T(8,128)} %param.967) | copy-start | bytes 393220
  327.2 1.9 copy-start.5
  596.1 566.8 %reduce-scatter.5.cloned.1.call-start = ((), (), s32[]{:S(2)}) async-start(), calls=%async_computation.3 | async-start | bytes 270336 | tf_op jit(solution)/shard_map/reduce_scatter | solution.py:141
  730.3 3.6 collective-permute-start
  734.6 4.6 collective-permute-start.1
  739.2 1.2 collective-permute-start.2
  740.5 4.0 collective-permute-start.3
  744.5 4.3 collective-permute-start.4
  757.8 1.9 copy-start.4
  1163.5 3.6 collective-permute-start.5
  1167.9 4.6 collective-permute-start.6
  1172.5 1.2 collective-permute-start.7
  1173.8 4.0 collective-permute-start.8
  1177.8 4.3 collective-permute-start.9
  1191.1 1.9 copy-start.3
  1441.2 5.7 copy-start.1
Sparse Core Ops, SparseCore 0:
  53.8 137.5 all-reduce.11
  596.2 133.3 reduce-scatter.2
  1029.4 133.3 reduce-scatter.4
